TPU v7x, 32 devices: a whole 2x2x4 slice. The times are simulated.
32 devices in a mesh: tmpl: 4 (over y, core), seq: 2 (over x), tp: 4 (over z).
Axes of the slice: x: 2, y: 2, z: 4, core: 2. Of those that a mesh axis runs over, the one named last changes fastest.
Arguments:
- tokens: bfloat16 [3072, 5376], P(('tmpl', 'seq', 'tp')), parts along dimension 0, may hold values from -6 to 6
- lengths: int32 [8], P('tmpl'), parts along dimension 0, may hold values from 1 to 384, as said below
- input_gain: float32 [5376], replicated, may hold values from 0.1 to 1.9
- query_proj: bfloat16 [5376, 512], P(None, 'tp'), may hold values from -0.078125 to 0.078125
- key_value: bfloat16 [5376, 1024], P(None, 'tp'), may hold values from -0.078125 to 0.078125
- query_gain: float32 [128], replicated, may hold values from 0.5 to 20, as said below
- key_gain: float32 [128], replicated, may hold values from 0.5 to 6, as said below
- window_cache: bfloat16 [4096, 1024], P(('tmpl', 'seq'), 'tp'), parts along dimension 0, may hold values from -6 to 6
- output_proj: bfloat16 [512, 5376], P('tp', 'seq'), may hold values from -0.25 to 0.25
- post_gain: float32 [5376], replicated, may hold values from 0.1 to 1.9
Outputs:
- layer_out: bfloat16 [3072, 5376], P(('tmpl', 'seq', 'tp')), parts along dimension 0
There are 4 independent parts, one for each index of `tmpl`. A program takes and returns all parts, laid end to end along the dimension named above; an argument that names none is the same for every part. Nothing has to cross between parts.
Inputs may be any that keep to these rules, and one draw needn't show every extreme that they name: The template's live slab tokens fill the first lengths[s] slots of seq index s, in order of s; one entry equals 384. `query_gain`: positive entries. `key_gain`: positive entries.
All inputs are finite; a program needn't handle non-finite values.
Results may differ from a plain program's by a relative error of at most 0.018.
The roundings to bfloat16 on the way count: a program that leaves them out, or rounds other values in their place, can miss the bound.
Values may be sent and summed in bfloat16 or wider, within the bound.
A program may use at most 64 MiB of HBM per device.

v0:
```python
import jax
import jax.numpy as jnp
from jax import lax
from jax.sharding import PartitionSpec as P

WIN = 1024
PREFIX = 32768
EPSILON = 1e-06
ROPE_BASE = 10000.0
QUERY_SCALE = 168.0 ** (-0.5)
MASKED = -1e30


def normalize(values, scale_gain):
    values = values.astype(jnp.float32)
    return (
        values * lax.rsqrt(jnp.mean(values * values, axis=-1, keepdims=True) + EPSILON) * scale_gain
    )


def rotate(values, positions):
    half_width = values.shape[-1] // 2
    frequency = jnp.power(
        ROPE_BASE, -2.0 * jnp.arange(half_width, dtype=jnp.float32) / values.shape[-1]
    )
    angles = positions.astype(jnp.float32)[:, None] * frequency[None, :]
    cosine_table = jnp.cos(angles)
    sine_table = jnp.sin(angles)
    first_half = values[:, :half_width]
    second_half = values[:, half_width:]
    return jnp.concatenate(
        [
            first_half * cosine_table - second_half * sine_table,
            second_half * cosine_table + first_half * sine_table,
        ],
        axis=1,
    )


def shards(
    tokens,
    lengths,
    input_gain,
    query_proj,
    key_value,
    query_gain,
    key_gain,
    window_cache,
    output_proj,
    post_gain,
):
    row_count = tokens.shape[0]
    slab_slots = row_count * lax.axis_size("tp")
    head_width = query_proj.shape[1]
    cache_slots = window_cache.shape[0]
    block_rows = slab_slots + cache_slots
    shard_count = lengths.shape[0]
    shard_index = lax.axis_index("seq")
    normed = normalize(tokens, input_gain).astype(jnp.bfloat16)
    piece = lax.all_gather(normed, "tp", axis=0, tiled=True)
    projected = jnp.concatenate(
        [
            jnp.dot(piece, query_proj, preferred_element_type=jnp.float32),
            jnp.dot(piece, key_value, preferred_element_type=jnp.float32),
        ],
        axis=1,
    )
    offsets = jnp.cumsum(lengths) - lengths
    shard_ids = jnp.arange(shard_count, dtype=jnp.int32)
    own_length = jnp.sum(jnp.where(shard_ids == shard_index, lengths, 0))
    own_offset = jnp.sum(jnp.where(shard_ids == shard_index, offsets, 0))
    slot_index = jnp.arange(slab_slots, dtype=jnp.int32)
    positions = PREFIX + own_offset + slot_index
    live_rows = slot_index < own_length
    queries = (
        rotate(normalize(projected[:, :head_width], query_gain), positions) * QUERY_SCALE
    ).astype(jnp.bfloat16)
    new_keys = rotate(
        normalize(projected[:, head_width : 2 * head_width], key_gain), positions
    ).astype(jnp.bfloat16)
    new_values = projected[:, 2 * head_width :].astype(jnp.bfloat16)
    own_block = jnp.concatenate(
        [jnp.concatenate([new_keys, new_values], axis=1), window_cache], axis=0
    )
    gathered = lax.all_gather(own_block, "seq", axis=0, tiled=True)
    running_max = jnp.full((slab_slots,), MASKED, jnp.float32)
    key_rows = gathered[:, :head_width]
    value_rows = gathered[:, head_width:]
    key_index = 0 + jnp.arange(gathered.shape[0], dtype=jnp.int32)
    key_shard = key_index // block_rows
    inner_row = key_index % block_rows
    picked = key_shard[:, None] == shard_ids[None, :]
    shard_offset = jnp.sum(jnp.where(picked, offsets[None, :], 0), axis=1)
    shard_length = jnp.sum(jnp.where(picked, lengths[None, :], 0), axis=1)
    in_slab = inner_row < slab_slots
    key_position = jnp.where(
        in_slab,
        PREFIX + shard_offset + inner_row,
        PREFIX - WIN + key_shard * cache_slots + inner_row - slab_slots,
    )
    key_live = jnp.where(in_slab, inner_row < shard_length, True)
    key_position, key_live = (key_position, key_live)
    visible = (
        key_live[None, :]
        & (key_position[None, :] <= positions[:, None])
        & (key_position[None, :] > positions[:, None] - WIN)
    )
    scores = lax.dot_general(
        queries, key_rows, (((1,), (1,)), ((), ())), preferred_element_type=jnp.float32
    )
    scores = jnp.where(visible, scores, MASKED)
    new_max = jnp.maximum(running_max, jnp.max(scores, axis=1))
    weights = jnp.where(visible, jnp.exp(scores - new_max[:, None]), 0.0)
    running_sum = jnp.sum(weights, axis=1)
    running_acc = jnp.dot(
        weights.astype(jnp.bfloat16), value_rows, preferred_element_type=jnp.float32
    )
    head_out = running_acc / jnp.where(live_rows, running_sum, 1.0)[:, None]
    head_out = jnp.where(live_rows[:, None], head_out, 0.0).astype(jnp.bfloat16)
    full_weights = lax.all_gather(output_proj, "seq", axis=1, tiled=True)
    projection = lax.psum_scatter(
        jnp.dot(head_out, full_weights, preferred_element_type=jnp.float32).astype(jnp.bfloat16),
        "tp",
        scatter_dimension=0,
        tiled=True,
    ).astype(jnp.float32)
    post_norm = normalize(projection, post_gain)
    return (tokens.astype(jnp.float32) + post_norm).astype(jnp.bfloat16)


def solution(mesh):
    return jax.shard_map(
        shards,
        mesh=mesh,
        in_specs=(
            P(("tmpl", "seq", "tp"), None),
            P("tmpl"),
            P(),
            P(None, "tp"),
            P(None, "tp"),
            P(),
            P(),
            P(("tmpl", "seq"), "tp"),
            P("tp", "seq"),
            P(),
        ),
        out_specs=P(("tmpl", "seq", "tp"), None),
        check_vma=False,
    )
```

profile of v0, /device:TPU:0, one launch (start us, length us, event | category | flops | bytes accessed | tf_op | source)
XLA Modules:
  0.0 221.9 jit_solution(13530554699072405083)
XLA Ops:
  6.5 0.0 copy-start
  6.5 0.0 copy-start.7
  6.5 0.0 all-gather.3.cloned.1.call-start
  6.5 1.7 fusion.2
  8.2 2.5 %fusion.4 = bf16[96,5376]{1,0:T(8,128)(2,1)} fusion(bf16[96,5376]{1,0:T(8,128)(2,1)} %param.10, f32[5376]{0:T(1024)} %param.12, f32[96]{0:T(128)S(1)} %add_rsqrt_fusion.3), kind=kLoop, calls=%fused_computation.13 | loop fusion | flops 2064384 | bytes 2086272 | tf_op jit(solution)/shard_map/convert_element_type | solution.py:59
  10.7 0.0 all-gather.3.cloned.1.call-update
  10.8 0.0 all-gather.5.cloned.1.call-start
  10.8 0.7 all-gather.5.cloned.1.call-update
  11.5 0.0 reduce-scatter.2.cloned.1.call-start
  11.6 0.0 copy-done.7
  11.6 0.2 reduce-window.9
  11.8 0.7 fusion.57
  13.2 0.6 iota_compare_fusion.1
  13.8 0.1 select_reduce_fusion.1
  14.0 79.3 %all-gather.3.cloned.1.call-done = bf16[384,5376]{1,0:T(8,128)(2,1)} async-done(((bf16[96,5376]{1,0:T(8,128)(2,1)}), bf16[384,5376]{1,0:T(8,128)(2,1)}) %all-gather.3.cloned.1.call-update) | async-done | bytes 4128784 | tf_op jit(solution)/shard_map/all_gather | solution.py:60
  93.3 0.0 copy-done
  93.3 0.0 copy-start.1
  93.3 0.0 copy-start.3
  93.3 4.0 %fusion.63 = f32[384,256]{0,1:T(8,128)S(1)} fusion(bf16[384,5376]{1,0:T(8,128)(2,1)} %all-gather.3.cloned.1.call-done, bf16[5376,256]{1,0:T(8,128)(2,1)S(1)} %copy-done), kind=kOutput, calls=%fused_computation.91 | convolution fusion | flops 1056964608 | bytes 7274496 | tf_op jit(solution)/shard_map/dot_general | solution.py:64
  97.3 0.0 copy-done.1
  97.3 0.0 copy-done.3
  97.3 0.0 copy-start.8
  97.3 0.0 copy-start.9
  97.4 0.0 copy-start.5
  97.4 1.3 multiply_reduce_fusion.1
  98.7 0.0 copy-done.8
  98.7 0.0 copy-done.9
  98.7 0.1 multiply_multiply_fusion
  98.8 1.1 fusion.35
  100.0 0.1 copy.12
  100.1 0.0 copy-done.5
  100.2 23.1 %all_gather.10 = bf16[1792,256]{1,0:T(8,128)(2,1)S(1)} all-gather(bf16[896,256]{1,0:T(8,128)(2,1)S(1)} %pad_maximum_fusion), channel_id=1, replica_groups=mesh['tmpl'=4,'seq'=2,'tp'=4] {'seq'}, dimensions={0}, use_global_device_ids=true | all-gather | bytes 1376256 | tf_op jit(solution)/shard_map/all_gather | solution.py:85
  123.3 0.0 copy-start.4
  123.3 0.9 copy-done.4
  124.2 2.0 fusion.62
  126.3 0.0 copy-start.2
  126.3 1.5 copy-done.2
  127.8 1.2 fusion.6
  129.0 0.6 broadcast_select_fusion
  129.7 0.0 all-gather.5.cloned.1.call-done
  129.7 6.9 %convolution_convert_fusion = bf16[384,5376]{1,0:T(8,128)(2,1)} fusion(bf16[128,5376]{1,0:T(8,128)(2,1)} %all-gather.5.cloned.1.call-done, f32[384,1792]{1,0:T(8,128)} %copy-done.2, f32[384]{0:T(512)S(1)} %broadcast_maximum_fusion, bf16[1792,256]{1,0:T(8,128)(2,1)} %copy-done.4, f32[384]{0:T(512)S(1)} %broadcast_select_fusion, ...), kind=kOutput, calls=%fused_computation | convolution fusion | flops 711671808 | bytes 8731776 | tf_op jit(solution)/shard_map/dot_general | solution.py:122
  136.6 0.0 copy-start.6
  136.6 0.0 reduce-scatter.2.cloned.1.call-update
  136.6 74.3 %reduce-scatter.2.cloned.1.call-done = bf16[96,5376]{1,0:T(8,128)(2,1)} async-done(((bf16[384,5376]{1,0:T(8,128)(2,1)}), bf16[96,5376]{1,0:T(8,128)(2,1)}) %reduce-scatter.2.cloned.1.call-update) | async-done | bytes 1032208 | tf_op jit(solution)/shard_map/reduce_scatter | solution.py:121
  210.9 1.5 fusion
  212.4 0.0 copy-done.6
  212.4 2.9 %fusion.5 = bf16[96,5376]{1,0:T(8,128)(2,1)} fusion(bf16[96,5376]{1,0:T(8,128)(2,1)} %reduce-scatter.2.cloned.1.call-done, bf16[96,5376]{1,0:T(8,128)(2,1)} %param.10, f32[5376]{0:T(1024)S(1)} %copy-done.6, f32[96]{0:T(128)S(1)} %add_rsqrt_fusion.2), kind=kLoop, calls=%fused_computation.14 | loop fusion | flops 3096576 | bytes 3118464 | tf_op jit(solution)/shard_map/convert_element_type | solution.py:128
  (15 shorter events, 0.2 us)
Async XLA Ops:
  6.5 86.8 %copy-start = (bf16[5376,256]{1,0:T(8,128)(2,1)S(1)}, bf16[5376,256]{1,0:T(8,128)(2,1)}, u32[]{:S(2)}) copy-start(bf16[5376,256]{1,0:T(8,128)(2,1)} %param.14) | copy-start | bytes 8257540
  6.5 5.0 %copy-start.7 = (s32[2]{0:T(128)S(1)}, s32[2]{0:T(128)}, u32[]{:S(2)}) copy-start(s32[2]{0:T(128)} %param.11) | copy-start | bytes 28
  6.5 86.8 %all-gather.3.cloned.1.call-start = ((), (), s32[]{:S(2)}) async-start(), calls=%async_computation.1 | async-start | bytes 5160960 | tf_op jit(solution)/shard_map/all_gather | solution.py:60
  10.8 118.9 %all-gather.5.cloned.1.call-start = ((), (), s32[]{:S(2)}) async-start(), calls=%async_computation.2 | async-start | bytes 2064384 | tf_op jit(solution)/shard_map/all_gather | solution.py:120
  11.5 199.4 %reduce-scatter.2.cloned.1.call-start = ((), (), s32[]{:S(2)}) async-start(), calls=%async_computation.3 | async-start | bytes 5160960 | tf_op jit(solution)/shard_map/reduce_scatter | solution.py:121
  93.3 4.0 %copy-start.1 = (bf16[384,5376]{1,0:T(8,128)(2,1)S(1)}, bf16[384,5376]{1,0:T(8,128)(2,1)}, u32[]{:S(2)}) copy-start(bf16[384,5376]{1,0:T(8,128)(2,1)} %all-gather.3.cloned.1.call-done) | copy-start | bytes 12386308
  93.3 4.0 %copy-start.3 = (bf16[5376,128]{1,0:T(8,128)(2,1)S(1)}, bf16[5376,128]{1,0:T(8,128)(2,1)}, u32[]{:S(2)}) copy-start(bf16[5376,128]{1,0:T(8,128)(2,1)} %param.13) | copy-start | bytes 4128772
  97.3 1.4 copy-start.8
  97.3 1.4 copy-start.9
  97.4 2.8 %copy-start.5 = (bf16[512,256]{1,0:T(8,128)(2,1)S(1)}, bf16[512,256]{1,0:T(8,128)(2,1)}, u32[]{:S(2)}) copy-start(bf16[512,256]{1,0:T(8,128)(2,1)} %param.17) | copy-start | bytes 786436
  123.3 0.9 copy-start.4
  126.3 1.5 copy-start.2
  136.6 75.8 %copy-start.6 = (f32[5376]{0:T(1024)S(1)}, f32[5376]{0:T(1024)}, u32[]{:S(2)}) copy-start(f32[5376]{0:T(1024)} %param.19) | copy-start | bytes 64516
Sparse Core Ops, SparseCore 0:
  10.9 82.3 all-gather.2
  94.8 33.0 all-gather.4
  136.7 74.1 reduce-scatter.1
where the time goes:
time: 222 us
  waiting for transfers between devices  154 us (69%)
  blocking collectives  23.1 us (10%)
  matrix products  14.2 us (6%)
  between operations  14 us (6%)
  other arithmetic  13.5 us (6%)
  local copies, waits for them, and re-layouts  2.63 us (1%)
    all_gather x1, waiting for transfers between devices, shards(): piece = lax.all_gather(normed, 'tp', axis=0, tiled=True)  79.3 us
    reduce_scatter x1, waiting for transfers between devices, shards(): lax.psum_scatter(jnp.dot(head_out, full_weights, preferred_element_type=j...  74.3 us
    all_gather x1, blocking collectives, shards(): gathered = lax.all_gather(own_block, 'seq', axis=0, tiled=True)  23.1 us
    dot_general x1, matrix products, shards(): jnp.dot(head_out, full_weights, preferred_element_type=jnp.float32)  6.89 us
  transfers between devices with their start and end apart: 3, of which 2 were waited for; matrix products, arithmetic and copies ran while one was open for 6% of the time, Pallas kernels for 0%

commit v1 on v0

--- a/solution.py
+++ b/solution.py
@@ -57,7 +57,12 @@
     shard_count = lengths.shape[0]
     shard_index = lax.axis_index("seq")
     normed = normalize(tokens, input_gain).astype(jnp.bfloat16)
-    piece = lax.all_gather(normed, "tp", axis=0, tiled=True)
+    ring = [normed]
+    for hop in range(3):
+        ring.append(lax.ppermute(ring[-1], "tp", [(dev, (dev + 1) % 4) for dev in range(4)]))
+    piece = jnp.roll(
+        jnp.concatenate(ring[::-1], axis=0), (lax.axis_index("tp") + 1) * ring[0].shape[0], axis=0
+    )
     projected = jnp.concatenate(
         [
             jnp.dot(piece, query_proj, preferred_element_type=jnp.float32),

time: 222 us -> 212 us (0.955)
  blocking collectives: 23.1 us -> 10.8 us
  local copies, waits for them, and re-layouts: 2.63 us -> 10.4 us
  waiting for transfers between devices: 154 us -> 147 us
  starting transfers between devices: 0.08 us -> 3.15 us
    all_gather x1 -> x0, waiting for transfers between devices: 79.3 us -> none  [shards(): piece = lax.all_gather(normed, 'tp', axis=0, tiled=True)]
    ppermute x0 -> x3, waiting for transfers between devices: none -> 73.7 us  [shards(): lax.ppermute(ring[-1], 'tp', [(dev, (dev + 1) % 4) for dev in range(4)])]
    all_gather x1, blocking collectives: 23.1 us -> 10.8 us  [shards(): gathered = lax.all_gather(own_block, 'seq', axis=0, tiled=True)]
    unnamed x20 -> x28, local copies, waits for them, and re-layouts: 2.47 us -> 10.3 us
    ppermute x0 -> x3, starting transfers between devices: none -> 3.11 us  [shards(): lax.ppermute(ring[-1], 'tp', [(dev, (dev + 1) % 4) for dev in range(4)])]
    dot_general x1, matrix products: 3.95 us -> 1.69 us  [shards(): jnp.dot(piece, key_value, preferred_element_type=jnp.float32)]
  transfers between devices with their start and end apart: 3 -> 5, of which waited for: 2 -> 4; matrix products, arithmetic and copies ran while one was open for 6% -> 9% of each run, Pallas kernels for 0% -> 0%
where the time goes in v1:
time: 212 us; the launch traced here: 211 us
  waiting for transfers between devices  147 us (69%)
  between operations  14.4 us (7%)
  other arithmetic  13.2 us (6%)
  matrix products  12.1 us (6%)
  blocking collectives  10.8 us (5%)
  local copies, waits for them, and re-layouts  10.4 us (5%)
  starting transfers between devices  3.15 us (1%)
    ppermute x3, waiting for transfers between devices, shards(): lax.ppermute(ring[-1], 'tp', [(dev, (dev + 1) % 4) for dev in range(4)])  73.7 us
    reduce_scatter x1, waiting for transfers between devices, shards(): lax.psum_scatter(jnp.dot(head_out, full_weights, preferred_element_type=j...  73.4 us
    all_gather x1, blocking collectives, shards(): gathered = lax.all_gather(own_block, 'seq', axis=0, tiled=True)  10.8 us
    unnamed x28, local copies, waits for them, and re-layouts  10.3 us
    dot_general x1, matrix products, shards(): jnp.dot(head_out, full_weights, preferred_element_type=jnp.float32)  6.84 us
  transfers between devices with their start and end apart: 5, of which 4 were waited for; matrix products, arithmetic and copies ran while one was open for 9% of the time, Pallas kernels for 0%

profile of v1, /device:TPU:0, one launch (start us, length us, event | category | flops | bytes accessed | tf_op | source)
XLA Modules:
  0.0 211.2 jit_solution(3976678394375951777)
XLA Ops:
  6.5 1.7 fusion.6
  8.2 1.5 fusion.8
  9.8 3.1 %collective-permute-start = (bf16[96,5376]{1,0:T(8,128)(2,1)S(1)}, bf16[96,5376]{1,0:T(8,128)(2,1)}, u32[]{:S(2)}, u32[]{:S(2)}) collective-permute-start(bf16[96,5376]{1,0:T(8,128)(2,1)S(1)} %fusion.8), channel_id=1, source_target_pairs={{0,1},{1,2},{2,3},{3,0},{4,5},{5,6},{6,7},{7,4},{8,9},{9,10},{10,1... | collective-permute-start | bytes 3096584 | tf_op jit(solution)/shard_map/ppermute | solution.py:62
  12.9 24.9 %collective-permute-done = bf16[96,5376]{1,0:T(8,128)(2,1)} collective-permute-done((bf16[96,5376]{1,0:T(8,128)(2,1)S(1)}, bf16[96,5376]{1,0:T(8,128)(2,1)}, u32[]{:S(2)}, u32[]{:S(2)}) %collective-permute-start) | collective-permute-done | bytes 1032224 | tf_op jit(solution)/shard_map/ppermute | solution.py:62
  37.8 0.0 collective-permute-start.1
  37.8 0.0 all-gather.2.cloned.1.call-update
  37.8 0.0 reduce-scatter.2.cloned.1.call-start
  37.9 0.2 reduce-window.9
  38.1 0.7 fusion.61
  38.8 25.1 %collective-permute-done.1 = bf16[96,5376]{1,0:T(8,128)(2,1)} collective-permute-done((bf16[96,5376]{1,0:T(8,128)(2,1)}, bf16[96,5376]{1,0:T(8,128)(2,1)}, u32[]{:S(2)}, u32[]{:S(2)}) %collective-permute-start.1) | collective-permute-done | bytes 1032224 | tf_op jit(solution)/shard_map/ppermute | solution.py:62
  63.9 0.0 collective-permute-start.2
  64.6 0.7 iota_compare_fusion.1
  65.3 0.1 select_reduce_fusion.1
  65.5 0.0 copy-start.1
  65.5 0.0 copy-start.5
  65.5 23.6 %collective-permute-done.2 = bf16[96,5376]{1,0:T(8,128)(2,1)} collective-permute-done((bf16[96,5376]{1,0:T(8,128)(2,1)}, bf16[96,5376]{1,0:T(8,128)(2,1)}, u32[]{:S(2)}, u32[]{:S(2)}) %collective-permute-start.2) | collective-permute-done | bytes 1032224 | tf_op jit(solution)/shard_map/ppermute | solution.py:62
  89.1 1.3 constant_dynamic-update-slice_fusion.7
  90.4 1.3 constant_dynamic-update-slice_fusion.6
  91.7 1.3 constant_dynamic-update-slice_fusion.5
  93.0 0.0 copy-done.1
  93.0 0.0 copy-done.5
  93.0 0.3 constant_dynamic-update-slice_fusion.4
  93.3 1.3 constant_dynamic-update-slice_fusion.3
  94.6 1.3 constant_dynamic-update-slice_fusion.2
  95.9 1.3 constant_dynamic-update-slice_fusion.1
  97.2 0.3 constant_dynamic-update-slice_fusion
  97.5 0.0 copy-done
  97.5 0.0 copy-start.10
  97.5 1.7 fusion
  99.3 0.0 copy-start.8
  99.3 0.0 copy-start.9
  99.3 0.0 copy-start.4
  99.4 1.5 multiply_reduce_fusion.1
  100.9 0.1 multiply_multiply_fusion
  101.0 1.1 fusion.39
  102.1 0.1 copy.12
  102.3 10.8 %all_gather.6 = bf16[1792,256]{1,0:T(8,128)(2,1)S(1)} all-gather(bf16[896,256]{1,0:T(8,128)(2,1)S(1)} %pad_maximum_fusion), channel_id=1, replica_groups=mesh['tmpl'=4,'seq'=2,'tp'=4] {'seq'}, dimensions={0}, use_global_device_ids=true | all-gather | bytes 1376256 | tf_op jit(solution)/shard_map/all_gather | solution.py:90
  113.1 0.9 copy-done.3
  114.1 2.0 fusion.68
  116.1 1.6 copy-done.2
  117.7 1.2 fusion.10
  118.9 0.7 broadcast_select_fusion
  119.6 0.0 all-gather.2.cloned.1.call-done
  119.6 6.8 %convolution_convert_fusion = bf16[384,5376]{1,0:T(8,128)(2,1)} fusion(bf16[128,5376]{1,0:T(8,128)(2,1)} %all-gather.2.cloned.1.call-done, f32[384,1792]{1,0:T(8,128)} %copy-done.2, f32[384]{0:T(512)S(1)} %broadcast_maximum_fusion, bf16[1792,256]{1,0:T(8,128)(2,1)} %copy-done.3, f32[384]{0:T(512)S(1)} %broadcast_select_fusion, ...), kind=kOutput, calls=%fused_computation | convolution fusion | flops 711671808 | bytes 8731776 | tf_op jit(solution)/shard_map/dot_general | solution.py:127
  126.5 0.0 reduce-scatter.2.cloned.1.call-update
  126.5 73.4 %reduce-scatter.2.cloned.1.call-done = bf16[96,5376]{1,0:T(8,128)(2,1)} async-done(((bf16[384,5376]{1,0:T(8,128)(2,1)}), bf16[96,5376]{1,0:T(8,128)(2,1)}) %reduce-scatter.2.cloned.1.call-update) | async-done | bytes 1032208 | tf_op jit(solution)/shard_map/reduce_scatter | solution.py:126
  199.9 1.5 fusion.4
  201.5 2.9 %fusion.9 = bf16[96,5376]{1,0:T(8,128)(2,1)} fusion(bf16[96,5376]{1,0:T(8,128)(2,1)} %reduce-scatter.2.cloned.1.call-done, bf16[96,5376]{1,0:T(8,128)(2,1)} %param.10, f32[5376]{0:T(1024)S(1)} %copy-done.6, f32[96]{0:T(128)S(1)} %add_rsqrt_fusion.2), kind=kLoop, calls=%fused_computation.18 | loop fusion | flops 3096576 | bytes 3118464 | tf_op jit(solution)/shard_map/convert_element_type | solution.py:133
  (27 shorter events, 0.2 us)
Async XLA Ops:
  6.5 91.0 %copy-start = (bf16[5376,256]{1,0:T(8,128)(2,1)S(1)}, bf16[5376,256]{1,0:T(8,128)(2,1)}, u32[]{:S(2)}) copy-start(bf16[5376,256]{1,0:T(8,128)(2,1)} %param.14) | copy-start | bytes 8257540
  6.5 31.4 %copy-start.7 = (s32[2]{0:T(128)S(1)}, s32[2]{0:T(128)}, u32[]{:S(2)}) copy-start(s32[2]{0:T(128)} %param.11) | copy-start | bytes 28
  6.5 113.1 %all-gather.2.cloned.1.call-start = ((), (), s32[]{:S(2)}) async-start(), calls=%async_computation.1 | async-start | bytes 2064384 | tf_op jit(solution)/shard_map/all_gather | solution.py:125
  9.8 28.0 %collective-permute-start = (bf16[96,5376]{1,0:T(8,128)(2,1)S(1)}, bf16[96,5376]{1,0:T(8,128)(2,1)}, u32[]{:S(2)}, u32[]{:S(2)}) collective-permute-start(bf16[96,5376]{1,0:T(8,128)(2,1)S(1)} %fusion.8), channel_id=1, source_target_pairs={{0,1},{1,2},{2,3},{3,0},{4,5},{5,6},{6,7},{7,4},{8,9},{9,10},{10,1... | collective-permute-start | bytes 3096584 | tf_op jit(solution)/shard_map/ppermute | solution.py:62
  37.8 26.1 %collective-permute-start.1 = (bf16[96,5376]{1,0:T(8,128)(2,1)}, bf16[96,5376]{1,0:T(8,128)(2,1)}, u32[]{:S(2)}, u32[]{:S(2)}) collective-permute-start(bf16[96,5376]{1,0:T(8,128)(2,1)} %collective-permute-done), channel_id=1, source_target_pairs={{0,1},{1,2},{2,3},{3,0},{4,5},{5,6},{6,7},{7,4},{8,9},{9,10},{10,1... | collective-permute-start | bytes 3096584 | tf_op jit(solution)/shard_map/ppermute | solution.py:62
  37.8 162.1 %reduce-scatter.2.cloned.1.call-start = ((), (), s32[]{:S(2)}) async-start(), calls=%async_computation.2 | async-start | bytes 5160960 | tf_op jit(solution)/shard_map/reduce_scatter | solution.py:126
  63.9 25.2 %collective-permute-start.2 = (bf16[96,5376]{1,0:T(8,128)(2,1)}, bf16[96,5376]{1,0:T(8,128)(2,1)}, u32[]{:S(2)}, u32[]{:S(2)}) collective-permute-start(bf16[96,5376]{1,0:T(8,128)(2,1)} %collective-permute-done.1), channel_id=1, source_target_pairs={{0,1},{1,2},{2,3},{3,0},{4,5},{5,6},{6,7},{7,4},{8,9},{9,10},{10,1... | collective-permute-start | bytes 3096584 | tf_op jit(solution)/shard_map/ppermute | solution.py:62
  65.5 27.5 %copy-start.1 = (bf16[96,5376]{1,0:T(8,128)(2,1)S(1)}, bf16[96,5376]{1,0:T(8,128)(2,1)}, u32[]{:S(2)}) copy-start(bf16[96,5376]{1,0:T(8,128)(2,1)} %param.10) | copy-start | bytes 3096580
  65.5 27.5 %copy-start.5 = (f32[5376]{0:T(1024)S(1)}, f32[5376]{0:T(1024)}, u32[]{:S(2)}) copy-start(f32[5376]{0:T(1024)} %param.12) | copy-start | bytes 64516
  97.5 1.8 copy-start.10
  99.3 1.6 copy-start.8
  99.3 1.6 copy-start.9
  99.3 2.9 %copy-start.4 = (bf16[512,256]{1,0:T(8,128)(2,1)S(1)}, bf16[512,256]{1,0:T(8,128)(2,1)}, u32[]{:S(2)}) copy-start(bf16[512,256]{1,0:T(8,128)(2,1)} %param.17) | copy-start | bytes 786436
  113.1 0.9 copy-start.3
  116.1 1.6 copy-start.2
  126.5 75.0 %copy-start.6 = (f32[5376]{0:T(1024)S(1)}, f32[5376]{0:T(1024)}, u32[]{:S(2)}) copy-start(f32[5376]{0:T(1024)} %param.19) | copy-start | bytes 64516
Sparse Core Ops, SparseCore 0:
  38.0 26.4 all-gather.1
  126.6 73.2 reduce-scatter.1
